TPU v7x, 32 devices: a whole 2x2x4 slice. The times are simulated.
32 devices in a mesh: seg: 2 (over x), rows: 16 (over z, y, core).
Axes of the slice: x: 2, y: 2, z: 4, core: 2. Of those that a mesh axis runs over, the one named last changes fastest.
Arguments:
- snapshots: float32 [512, 131072], P('seg', 'rows'), parts along dimension 0, may hold values from -400 to 400
Outputs:
- q_panel: float32 [64, 131072], P('seg', 'rows'), parts along dimension 0
- r_panel: float32 [64, 32], P('seg'), parts along dimension 0
- projected: float32 [64, 224], P('seg'), parts along dimension 0
- trailing: float32 [448, 131072], P('seg', 'rows'), parts along dimension 0
There are 2 independent parts, one for each index of `seg`. A program takes and returns all parts, laid end to end along the dimension named above; each array names one. Nothing has to cross between parts.
All inputs are finite; a program needn't handle non-finite values.
Results may differ from a plain program's by a relative error of at most 0.000082.
Values sent between devices are 32-bit elements; how exact they have to be, the bound alone decides.
A program may use at most 64 MiB of HBM per device.

v0:
```python
import jax
import jax.numpy as jnp
from jax import lax
from jax.sharding import PartitionSpec as P

PANEL = 32


def inner(left, right):
    return lax.dot_general(
        left,
        right,
        (((1,), (1,)), ((), ())),
        precision=lax.Precision.HIGHEST,
        preferred_element_type=jnp.float32,
    )


def local(snapshots):
    panel = snapshots[:PANEL]
    rest = snapshots[PANEL:]
    totals = lax.psum(inner(panel, snapshots), "rows")
    lower = jnp.linalg.cholesky(totals[:, :PANEL])
    q_panel = jax.scipy.linalg.solve_triangular(lower, panel, lower=True)
    projected = jax.scipy.linalg.solve_triangular(lower, totals[:, PANEL:], lower=True)
    update = lax.dot_general(
        projected,
        q_panel,
        (((0,), (0,)), ((), ())),
        precision=lax.Precision.HIGHEST,
        preferred_element_type=jnp.float32,
    )
    trailing = rest - update
    return (q_panel, lower.T, projected, trailing)


def solution(mesh):
    return jax.shard_map(
        local,
        mesh=mesh,
        in_specs=(P("seg", "rows"),),
        out_specs=(P("seg", "rows"), P("seg", None), P("seg", None), P("seg", "rows")),
        check_vma=False,
    )
```

profile of v0, /device:TPU:0, one launch (start us, length us, event | category | flops | bytes accessed | tf_op | source)
XLA Modules:
  0.0 94.1 jit_solution(7879214852546602777)
XLA Ops:
  0.6 9.2 %fusion.2 = f32[32,256]{0,1:T(8,128)S(1)} fusion(f32[256,8192]{1,0:T(8,128)} %param.1), kind=kOutput, calls=%fused_computation.3 | convolution fusion | flops 805306368 | bytes 9469952 | tf_op jit(solution)/shard_map/dot_general | solution.py:10
  9.8 63.8 %psum.7 = f32[32,256]{0,1:T(8,128)S(1)} all-reduce(f32[32,256]{0,1:T(8,128)S(1)} %fusion.2), channel_id=1, replica_groups=mesh['seg'=2,'rows'=16] {'rows'}, use_global_device_ids=true, to_apply=%region_0.0 | all-reduce | flops 8192 | bytes 65536 | tf_op jit(solution)/shard_map/psum | solution.py:22
  73.6 0.1 copy.6
  73.7 2.9 %cholesky.16 = f32[32,32]{1,0:T(8,128)S(1)} custom-call(f32[32,32]{1,0:T(8,128)S(1)} %fusion.8), custom_call_target="Cholesky" | custom-call | tf_op jit(solution)/shard_map/jit(cholesky)/cholesky | solution.py:23
  76.6 0.6 compare_reduce_fusion
  77.3 0.7 fusion.9
  78.0 0.7 copy.7
  78.6 2.4 %custom-call.10 = f32[1,32,32]{1,2,0:T(8,128)S(1)} custom-call(f32[1,32,32]{2,1,0:T(8,128)S(1)} %get-tuple-element.9), custom_call_target="InvertDiagBlocksLowerTriangular" | custom-call | tf_op jit(solution)/shard_map/jit(_solve_triangular)/triangular_solve | solution.py:24
  81.1 0.4 fusion.4
  81.4 0.0 copy-start.1
  81.4 2.3 %fusion = f32[32,8192]{1,0:T(8,128)S(1)} fusion(f32[256,8192]{1,0:T(8,128)} %param.1, f32[1,32,32]{1,2,0:T(8,128)S(1)} %custom-call.10), kind=kOutput, calls=%fused_computation.1 | convolution fusion | flops 100663296 | bytes 2101248 | tf_op jit(solution)/shard_map/jit(_solve_triangular)/triangular_solve | solution.py:24
  83.7 0.0 copy-start
  83.7 10.4 %convolution_subtract_fusion = f32[224,8192]{1,0:T(8,128)} fusion(f32[32,224]{1,0:T(8,128)S(1)} %fusion.4, f32[32,8192]{1,0:T(8,128)S(1)} %fusion, f32[256,8192]{1,0:T(8,128)} %param.1), kind=kOutput, calls=%fused_computation | convolution fusion | flops 706478080 | bytes 15757312 | tf_op jit(solution)/shard_map/dot_general | solution.py:26
  94.1 0.0 copy-done.1
  94.1 0.0 copy-done
  (3 shorter events, 0.0 us)
Async XLA Ops:
  81.4 12.7 %copy-start.1 = (f32[32,224]{1,0:T(8,128)}, f32[32,224]{1,0:T(8,128)S(1)}, u32[]{:S(2)}) copy-start(f32[32,224]{1,0:T(8,128)S(1)} %fusion.4) | copy-start | bytes 86020
  83.7 10.4 %copy-start = (f32[32,8192]{1,0:T(8,128)}, f32[32,8192]{1,0:T(8,128)S(1)}, u32[]{:S(2)}) copy-start(f32[32,8192]{1,0:T(8,128)S(1)} %fusion) | copy-start | bytes 3145732
where the time goes:
time: 94.3 us; the launch traced here: 94.1 us
  blocking collectives  63.8 us (68%)
  matrix products  22.2 us (24%)
  other arithmetic  6.69 us (7%)
    psum x1, blocking collectives, local(): totals = lax.psum(inner(panel, snapshots), 'rows')  63.8 us
    dot_general x1, matrix products, local(): lax.dot_general(projected, q_panel, (((0,), (0,)), ((), ())), precision=l...  10.4 us
    dot_general x1, matrix products, inner(): lax.dot_general(left, right, (((1,), (1,)), ((), ())), precision=lax.Prec...  9.17 us
    another operation x3, other arithmetic, local(): lower = jnp.linalg.cholesky(totals[:, :PANEL])  3.6 us
    another operation x1, other arithmetic, local(): q_panel = jax.scipy.linalg.solve_triangular(lower, panel, lower=True)  2.44 us
    another operation x1, matrix products, local(): q_panel = jax.scipy.linalg.solve_triangular(lower, panel, lower=True)  2.26 us

commit v1 on v0

--- a/solution.py
+++ b/solution.py
@@ -19,7 +19,7 @@
 def local(snapshots):
     panel = snapshots[:PANEL]
     rest = snapshots[PANEL:]
-    totals = lax.psum(inner(panel, snapshots), "rows")
+    totals = jnp.sum(jax.lax.all_gather(inner(panel, snapshots), "rows"), axis=0)
     lower = jnp.linalg.cholesky(totals[:, :PANEL])
     q_panel = jax.scipy.linalg.solve_triangular(lower, panel, lower=True)
     projected = jax.scipy.linalg.solve_triangular(lower, totals[:, PANEL:], lower=True)

time: 94.3 us -> 57 us (0.60)
  blocking collectives: 63.8 us -> 24.6 us
  matrix products: 22.2 us -> 24 us
    psum x1 -> x0, blocking collectives: 63.8 us -> none  [local(): totals = lax.psum(inner(panel, snapshots), 'rows')]
    all_gather x0 -> x1, blocking collectives: none -> 24.6 us  [local(): jax.lax.all_gather(inner(panel, snapshots), 'rows')]
    dot_general x1, matrix products: 9.17 us -> 11.1 us  [inner(): lax.dot_general(left, right, (((1,), (1,)), ((), ())), precision=lax.Prec...]
where the time goes in v1:
time: 57 us; the launch traced here: 56.8 us
  blocking collectives  24.6 us (43%)
  matrix products  24 us (42%)
  other arithmetic  6.72 us (12%)
  local copies, waits for them, and re-layouts  0.77 us (1%)
  between operations  0.69 us (1%)
    all_gather x1, blocking collectives, local(): jax.lax.all_gather(inner(panel, snapshots), 'rows')  24.6 us
    dot_general x1, matrix products, inner(): lax.dot_general(left, right, (((1,), (1,)), ((), ())), precision=lax.Prec...  11.1 us
    dot_general x1, matrix products, local(): lax.dot_general(projected, q_panel, (((0,), (0,)), ((), ())), precision=l...  10.4 us
    another operation x3, other arithmetic, local(): lower = jnp.linalg.cholesky(totals[:, :PANEL])  3.6 us
    another operation x1, other arithmetic, local(): q_panel = jax.scipy.linalg.solve_triangular(lower, panel, lower=True)  2.44 us
    another operation x1, matrix products, local(): q_panel = jax.scipy.linalg.solve_triangular(lower, panel, lower=True)  2.26 us

profile of v1, /device:TPU:0, one launch (start us, length us, event | category | flops | bytes accessed | tf_op | source)
XLA Modules:
  0.0 56.8 jit_solution(11678917172209085594)
XLA Ops:
  0.6 11.1 %fusion.2 = f32[32,256]{1,0:T(8,128)S(1)} fusion(f32[256,8192]{1,0:T(8,128)} %param.1), kind=kOutput, calls=%fused_computation.3 | convolution fusion | flops 805306368 | bytes 9469952 | tf_op jit(solution)/shard_map/dot_general | solution.py:10
  11.7 24.6 %all-gather = f32[512,256]{1,0:T(8,128)S(1)} all-gather(f32[32,256]{1,0:T(8,128)S(1)} %fusion.2), channel_id=2, replica_groups=mesh['seg'=2,'rows'=16] {'rows'}, dimensions={0}, use_global_device_ids=true | all-gather | bytes 557056 | tf_op jit(solution)/shard_map/all_gather | solution.py:22
  36.4 0.1 copy.10
  36.4 2.9 %cholesky.16 = f32[32,32]{1,0:T(8,128)S(1)} custom-call(f32[32,32]{1,0:T(8,128)S(1)} %fusion.8), custom_call_target="Cholesky" | custom-call | tf_op jit(solution)/shard_map/jit(cholesky)/cholesky | solution.py:23
  39.4 0.6 %compare_reduce_fusion = pred[]{:T(512)} fusion(f32[32]{0:T(128)S(1)} %select_reduce_fusion), kind=kLoop, calls=%fused_computation.17 | loop fusion | flops 63 | bytes 129 | tf_op jit(solution)/shard_map/jit(cholesky)/cholesky | solution.py:23
  40.0 0.7 %fusion.9 = (f32[32,32]{0,1:T(8,128)S(1)}, f32[1,32,32]{2,1,0:T(8,128)S(1)}) fusion(f32[32,32]{1,0:T(8,128)S(1)} %cholesky.16, pred[]{:T(512)} %compare_reduce_fusion), kind=kLoop, calls=%fused_computation.16 | loop fusion | flops 4096 | bytes 12289 | tf_op jit(solution)/shard_map/transpose | solution.py:34
  40.7 0.7 %copy.9 = f32[32,32]{1,0:T(8,128)} copy(f32[32,32]{0,1:T(8,128)S(1)} %get-tuple-element.12) | data formatting | bytes 8192
  41.4 2.4 %custom-call.10 = f32[1,32,32]{1,2,0:T(8,128)S(1)} custom-call(f32[1,32,32]{2,1,0:T(8,128)S(1)} %get-tuple-element.13), custom_call_target="InvertDiagBlocksLowerTriangular" | custom-call | tf_op jit(solution)/shard_map/jit(_solve_triangular)/triangular_solve | solution.py:24
  43.8 0.3 fusion.4
  44.1 0.0 copy-start.1
  44.1 2.3 %fusion = f32[32,8192]{1,0:T(8,128)S(1)} fusion(f32[256,8192]{1,0:T(8,128)} %param.1, f32[1,32,32]{1,2,0:T(8,128)S(1)} %custom-call.10), kind=kOutput, calls=%fused_computation.1 | convolution fusion | flops 100663296 | bytes 2101248 | tf_op jit(solution)/shard_map/jit(_solve_triangular)/triangular_solve | solution.py:24
  46.4 0.0 copy-start
  46.4 10.4 %convolution_subtract_fusion = f32[224,8192]{1,0:T(8,128)} fusion(f32[32,224]{1,0:T(8,128)S(1)} %fusion.4, f32[32,8192]{1,0:T(8,128)S(1)} %fusion, f32[256,8192]{1,0:T(8,128)} %param.1), kind=kOutput, calls=%fused_computation | convolution fusion | flops 706478080 | bytes 15757312 | tf_op jit(solution)/shard_map/dot_general | solution.py:26
  56.8 0.0 copy-done.1
  56.8 0.0 copy-done
  (4 shorter events, 0.1 us)
Async XLA Ops:
  44.1 12.7 %copy-start.1 = (f32[32,224]{1,0:T(8,128)}, f32[32,224]{1,0:T(8,128)S(1)}, u32[]{:S(2)}) copy-start(f32[32,224]{1,0:T(8,128)S(1)} %fusion.4) | copy-start | bytes 86020
  46.4 10.4 %copy-start = (f32[32,8192]{1,0:T(8,128)}, f32[32,8192]{1,0:T(8,128)S(1)}, u32[]{:S(2)}) copy-start(f32[32,8192]{1,0:T(8,128)S(1)} %fusion) | copy-start | bytes 3145732
